TPU v7x, 32 devices: a whole 2x2x4 slice. The times are simulated.
32 devices in a mesh: ta: 4 (over y, x), ha: 2 (over core), head: 4 (over z).
Axes of the slice: x: 2, y: 2, z: 4, core: 2. Of those that a mesh axis runs over, the one named last changes fastest.
Arguments:
- queries: bfloat16 [24, 16, 8, 2048], P('ta', ('ha', 'head')), may hold values from -90 to 90
- keys: bfloat16 [24, 16, 8, 2048], P('ta', ('ha', 'head')), may hold values from -4.5 to 4.5
- values: bfloat16 [24, 16, 8, 2048], P('ta', ('ha', 'head')), may hold values from -6 to 6
- out_grad: bfloat16 [24, 16, 8, 2048], P('ta', ('ha', 'head')), may hold values from -6 to 6
Outputs:
- attended: bfloat16 [24, 16, 8, 2048], P('ta', ('ha', 'head'))
- query_grad: bfloat16 [24, 16, 8, 2048], P('ta', ('ha', 'head'))
- key_grad: bfloat16 [24, 16, 8, 2048], P('ta', ('ha', 'head'))
- value_grad: bfloat16 [24, 16, 8, 2048], P('ta', ('ha', 'head'))
All inputs are finite; a program needn't handle non-finite values.
Results may differ from a plain program's by a relative error of at most 0.025.
Values may be sent and summed in bfloat16 or wider, within the bound.
A program may use at most 128 MiB of HBM per device.

v0:
```python
import math

import jax
import jax.numpy as jnp
from jax import lax
from jax.sharding import PartitionSpec as P

DH = 128


def padded(value, sides, width):
    for axis, dim in sides:
        size, length = (lax.axis_size(axis), value.shape[dim])
        up = [(i, (i + 1) % size) for i in range(size - 1)]
        down = [(j, i) for i, j in up]
        last = lax.slice_in_dim(value, length - width, length, axis=dim)
        leading = lax.slice_in_dim(value, 0, width, axis=dim)
        before = lax.ppermute(last, axis, up)
        after = lax.ppermute(leading, axis, down)
        value = jnp.concatenate([before, value, after], axis=dim)
    return value


def shifted(value, axis, by):
    size = lax.axis_size(axis)
    pairs = [(i, i + by) for i in range(size) if 0 <= i + by < size]
    return lax.ppermute(value, axis, pairs)


def body(queries, keys, values, out_grad):
    factor = 1.0 / math.sqrt(DH)
    local_queries, local_keys, local_values, local_grads = (
        lax.all_to_all(queries, "head", split_axis=3, concat_axis=1, tiled=True),
        lax.all_to_all(keys, "head", split_axis=3, concat_axis=1, tiled=True),
        lax.all_to_all(values, "head", split_axis=3, concat_axis=1, tiled=True),
        lax.all_to_all(out_grad, "head", split_axis=3, concat_axis=1, tiled=True),
    )
    frames, height, columns, local_width = local_queries.shape
    heads_local = local_width // DH
    tokens = frames * height * columns
    flat_queries = local_queries.reshape(tokens, local_width)
    flat_grads = local_grads.reshape(tokens, local_width)
    paired = jnp.stack([local_keys, local_values]).reshape(2, 1, 1, tokens, local_width)
    beside_all = padded(paired, (("ta", 1), ("ha", 2)), 1)
    near_keys = beside_all[0].reshape(9 * tokens, local_width)
    near_values = beside_all[1].reshape(9 * tokens, local_width)
    offsets = jnp.arange(3, dtype=jnp.int32) - 1
    time_place = lax.axis_index("ta") + offsets
    row_place = lax.axis_index("ha") + offsets
    time_valid = (time_place >= 0) & (time_place < lax.axis_size("ta"))
    row_valid = (row_place >= 0) & (row_place < lax.axis_size("ha"))
    key_valid = jnp.repeat((time_valid[:, None] & row_valid[None, :]).reshape(9), tokens)
    allowed = key_valid[None, :]
    attended_parts = []
    total_parts = []
    dot_parts = []
    qgrad_parts = []
    kpart_parts = []
    vpart_parts = []
    for head_id in range(heads_local):
        start_col = head_id * DH
        stop_col = start_col + DH
        query_rows = flat_queries[:, start_col:stop_col]
        grad_rows = flat_grads[:, start_col:stop_col]
        key_rows = near_keys[:, start_col:stop_col]
        value_rows = near_values[:, start_col:stop_col]
        scores = (
            jnp.einsum("qd,kd->qk", query_rows, key_rows, preferred_element_type=jnp.float32)
            * factor
        )
        scores = jnp.where(allowed, scores, -jnp.inf)
        highest = jnp.max(scores, axis=1, keepdims=True)
        log_total = highest + jnp.log(jnp.sum(jnp.exp(scores - highest), axis=1, keepdims=True))
        probs = jnp.where(allowed, jnp.exp(scores - log_total), 0.0)
        probs_low = probs.astype(jnp.bfloat16)
        attended_rows = jnp.einsum(
            "qk,kd->qd", probs_low, value_rows, preferred_element_type=jnp.float32
        ).astype(jnp.bfloat16)
        row_dot = jnp.sum(grad_rows.astype(jnp.float32) * attended_rows.astype(jnp.float32), axis=1)
        prob_grad = jnp.einsum(
            "qd,kd->qk", grad_rows, value_rows, preferred_element_type=jnp.float32
        )
        score_grad = (probs * (prob_grad - row_dot[:, None])).astype(jnp.bfloat16)
        query_rows_grad = (
            jnp.einsum("qk,kd->qd", score_grad, key_rows, preferred_element_type=jnp.float32)
            * factor
        ).astype(jnp.bfloat16)
        attended_parts.append(attended_rows)
        total_parts.append(log_total[:, 0])
        dot_parts.append(row_dot)
        qgrad_parts.append(query_rows_grad)
        value_part = jnp.einsum(
            "qk,qd->kd", probs_low, grad_rows, preferred_element_type=jnp.float32
        )
        key_part = (
            jnp.einsum("qk,qd->kd", score_grad, query_rows, preferred_element_type=jnp.float32)
            * factor
        )
        kpart_parts.append(key_part)
        vpart_parts.append(value_part)
    attended = jnp.concatenate(attended_parts, axis=1).reshape(frames, height, columns, local_width)
    query_grad = jnp.concatenate(qgrad_parts, axis=1).reshape(frames, height, columns, local_width)
    key_terms = jnp.concatenate(kpart_parts, axis=1)
    value_terms = jnp.concatenate(vpart_parts, axis=1)
    contrib = jnp.stack([key_terms, value_terms]).reshape(2, 3, 3, tokens, local_width)
    from_lower = shifted(contrib[:, 2], "ta", 1)
    from_upper = shifted(contrib[:, 0], "ta", -1)
    row_terms = contrib[:, 1] + from_lower + from_upper
    beside_lower = shifted(row_terms[:, 2], "ha", 1)
    beside_upper = shifted(row_terms[:, 0], "ha", -1)
    summed = row_terms[:, 1] + beside_lower + beside_upper
    key_grad = summed[0].reshape(frames, height, columns, local_width).astype(jnp.bfloat16)
    value_grad = summed[1].reshape(frames, height, columns, local_width).astype(jnp.bfloat16)
    return (
        lax.all_to_all(attended, "head", split_axis=1, concat_axis=3, tiled=True),
        lax.all_to_all(query_grad, "head", split_axis=1, concat_axis=3, tiled=True),
        lax.all_to_all(key_grad, "head", split_axis=1, concat_axis=3, tiled=True),
        lax.all_to_all(value_grad, "head", split_axis=1, concat_axis=3, tiled=True),
    )


def solution(mesh):
    in_specs = (
        P("ta", ("ha", "head"), None, None),
        P("ta", ("ha", "head"), None, None),
        P("ta", ("ha", "head"), None, None),
        P("ta", ("ha", "head"), None, None),
    )
    out_specs = (
        P("ta", ("ha", "head"), None, None),
        P("ta", ("ha", "head"), None, None),
        P("ta", ("ha", "head"), None, None),
        P("ta", ("ha", "head"), None, None),
    )
    return jax.shard_map(body, mesh=mesh, in_specs=in_specs, out_specs=out_specs, check_vma=False)
```

profile of v0, /device:TPU:0, one launch (start us, length us, event | category | flops | bytes accessed | tf_op | source)
XLA Modules:
  0.0 581.5 jit_solution(10598753241762434903)
XLA Ops:
  0.6 9.2 %copy.83 = bf16[6,2,8,2048]{2,0,1,3:T(8,128)(2,1)} copy(bf16[6,2,8,2048]{3,2,1,0:T(8,128)(2,1)} %param.5) | data formatting | bytes 786432 | tf_op args[1]
  9.9 9.6 %reshape.103 = bf16[4,2,24576]{2,1,0:T(2,128)(2,1)} reshape(bf16[2048,2,6,8]{3,2,1,0:T(8,128)(2,1)} %bitcast.90) | data formatting | bytes 786432
  19.5 6.3 %all-to-all-start = ((bf16[4,2,24576]{2,1,0:T(2,128)(2,1)}), bf16[4,2,24576]{2,1,0:T(2,128)(2,1)S(1)}, u32[]{:S(2)}, u32[]{:S(2)}) async-start(bf16[4,2,24576]{2,1,0:T(2,128)(2,1)} %reshape.103), calls=%async_computation | async-start | bytes 786432 | tf_op jit(solution)/shard_map/all_to_all | solution.py:34
  25.8 8.5 %copy.86 = bf16[6,2,8,2048]{2,0,1,3:T(8,128)(2,1)} copy(bf16[6,2,8,2048]{3,2,1,0:T(8,128)(2,1)S(1)} %copy-done.10) | data formatting | bytes 786432 | tf_op args[2]
  34.3 9.5 %reshape.101 = bf16[4,2,24576]{2,1,0:T(2,128)(2,1)} reshape(bf16[2048,2,6,8]{3,2,1,0:T(8,128)(2,1)} %bitcast.91) | data formatting | bytes 786432
  43.8 5.1 all-to-all-start.1
  48.9 9.4 %reshape.104 = bf16[2048,2,6,8]{3,2,1,0:T(8,128)(2,1)} reshape(bf16[4,2,24576]{2,1,0:T(2,128)(2,1)S(1)} %all-to-all-done) | data formatting | bytes 786432
  58.3 8.1 %copy.117 = bf16[6,2,8,4,512]{4,3,2,1,0:T(4,128)(2,1)S(1)} copy(bf16[6,2,8,4,512]{2,0,1,4,3:T(8,128)(2,1)} %bitcast.86) | data formatting | bytes 786432 | tf_op jit(solution)/shard_map/all_to_all | solution.py:34
  66.5 9.4 %reshape.102 = bf16[2048,2,6,8]{3,2,1,0:T(8,128)(2,1)} reshape(bf16[4,2,24576]{2,1,0:T(2,128)(2,1)S(1)} %all-to-all-done.1) | data formatting | bytes 786432
  75.9 8.1 %copy.118 = bf16[6,2,8,4,512]{4,3,2,1,0:T(4,128)(2,1)S(1)} copy(bf16[6,2,8,4,512]{2,0,1,4,3:T(8,128)(2,1)} %bitcast.87) | data formatting | bytes 786432 | tf_op jit(solution)/shard_map/all_to_all | solution.py:35
  85.5 4.6 collective-permute-start
  90.1 16.5 %collective-permute-done.1 = bf16[2,1,1,384,512]{4,3,2,1,0:T(8,128)(2,1)S(1)} collective-permute-done((bf16[2,1,1,384,512]{4,3,2,1,0:T(8,128)(2,1)S(1)}, bf16[2,1,1,384,512]{4,3,2,1,0:T(8,128)(2,1)S(1)}, u32[]{:S(2)}, u32[]{:S(2)}) %collective-permute-start.1) | collective-permute-done | bytes 786464 | tf_op jit(solution)/shard_map/ppermute | solution.py:19
  109.6 6.4 %collective-permute-start.2 = (bf16[2,3,1,384,512]{4,3,2,1,0:T(8,128)(2,1)}, bf16[2,3,1,384,512]{4,3,2,1,0:T(8,128)(2,1)}, u32[]{:S(2)}, u32[]{:S(2)}) collective-permute-start(bf16[2,3,1,384,512]{4,3,2,1,0:T(8,128)(2,1)} %pad_maximum_fusion.4), channel_id=1, source_target_pairs={{0,4},{1,5},{2,6},{3,7},{8,12},{9,13},{10,14},{11,15},{16,20},{17,... | collective-permute-start | bytes 7077896 | tf_op jit(solution)/shard_map/ppermute | solution.py:18
  116.0 9.2 %copy.89 = bf16[6,2,8,2048]{2,0,1,3:T(8,128)(2,1)} copy(bf16[6,2,8,2048]{3,2,1,0:T(8,128)(2,1)} %param.4) | data formatting | bytes 786432 | tf_op args[0]
  125.2 9.6 %reshape.105 = bf16[4,2,24576]{2,1,0:T(2,128)(2,1)} reshape(bf16[2048,2,6,8]{3,2,1,0:T(8,128)(2,1)} %bitcast.92) | data formatting | bytes 786432
  134.8 5.1 all-to-all-start.2
  139.9 8.5 %copy.95 = bf16[6,2,8,2048]{2,0,1,3:T(8,128)(2,1)} copy(bf16[6,2,8,2048]{3,2,1,0:T(8,128)(2,1)S(1)} %copy-done.11) | data formatting | bytes 786432 | tf_op args[3]
  148.4 9.5 %reshape.107 = bf16[4,2,24576]{2,1,0:T(2,128)(2,1)} reshape(bf16[2048,2,6,8]{3,2,1,0:T(8,128)(2,1)} %bitcast.93) | data formatting | bytes 786432
  158.0 5.1 all-to-all-start.4
  163.3 9.4 %reshape.106 = bf16[2048,2,6,8]{3,2,1,0:T(8,128)(2,1)} reshape(bf16[4,2,24576]{2,1,0:T(2,128)(2,1)S(1)} %all-to-all-done.2) | data formatting | bytes 786432
  172.7 8.1 %copy.119 = bf16[6,2,8,4,512]{4,3,2,1,0:T(4,128)(2,1)S(1)} copy(bf16[6,2,8,4,512]{2,0,1,4,3:T(8,128)(2,1)} %bitcast.88) | data formatting | bytes 786432 | tf_op jit(solution)/shard_map/all_to_all | solution.py:33
  181.0 10.5 %reshape.108 = bf16[2048,2,6,8]{3,2,1,0:T(8,128)(2,1)} reshape(bf16[4,2,24576]{2,1,0:T(2,128)(2,1)} %all-to-all-done.4) | data formatting | bytes 786432
  191.4 8.8 %copy.120 = bf16[6,2,8,4,512]{4,3,2,1,0:T(4,128)(2,1)} copy(bf16[6,2,8,4,512]{2,0,1,4,3:T(8,128)(2,1)} %bitcast.89) | data formatting | bytes 786432 | tf_op jit(solution)/shard_map/all_to_all | solution.py:36
  202.5 3.6 pad_maximum_fusion
  226.9 2.6 fusion.9
  230.6 2.7 fusion.10
  235.2 4.5 fusion.11
  239.8 4.5 fusion.8
  244.3 3.2 pad_maximum_fusion.2
  247.5 8.2 %copy.106 = f32[3456,512]{1,0:T(8,128)} copy(f32[3456,512]{0,1:T(8,128)} %pad_maximum_fusion.2) | data formatting | bytes 14155776 | tf_op jit(solution)/shard_map/concatenate | solution.py:104
  255.8 2.9 convolution_multiply_fusion.4
  260.5 3.3 pad_maximum_fusion.1
  263.8 8.2 %copy.105 = f32[3456,512]{1,0:T(8,128)} copy(f32[3456,512]{0,1:T(8,128)} %pad_maximum_fusion.1) | data formatting | bytes 14155776 | tf_op jit(solution)/shard_map/concatenate | solution.py:103
  271.9 4.4 fusion.13
  276.4 18.5 %collective-permute-start.4 = (f32[2,3,384,512]{3,2,1,0:T(8,128)S(1)}, f32[2,3,384,512]{3,2,1,0:T(8,128)}, u32[]{:S(2)}, u32[]{:S(2)}) collective-permute-start(f32[2,3,384,512]{3,2,1,0:T(8,128)S(1)} %get-tuple-element.4), channel_id=1, source_target_pairs={{0,8},{8,16},{16,24},{1,9},{9,17},{17,25},{2,10},{10,18},{18,26},{... | collective-permute-start | bytes 14155784 | tf_op jit(solution)/shard_map/ppermute | solution.py:27
  296.1 94.9 %collective-permute-done.4 = f32[2,3,384,512]{3,2,1,0:T(8,128)} collective-permute-done((f32[2,3,384,512]{3,2,1,0:T(8,128)S(1)}, f32[2,3,384,512]{3,2,1,0:T(8,128)}, u32[]{:S(2)}, u32[]{:S(2)}) %collective-permute-start.4) | collective-permute-done | bytes 4718624 | tf_op jit(solution)/shard_map/ppermute | solution.py:27
  391.0 105.1 %collective-permute-done.5 = f32[2,3,384,512]{3,2,1,0:T(8,128)} collective-permute-done((f32[2,3,384,512]{3,2,1,0:T(8,128)S(1)}, f32[2,3,384,512]{3,2,1,0:T(8,128)}, u32[]{:S(2)}, u32[]{:S(2)}) %collective-permute-start.5) | collective-permute-done | bytes 4718624 | tf_op jit(solution)/shard_map/ppermute | solution.py:27
  496.1 7.7 %fusion.17 = f32[2,3,384,512]{3,2,1,0:T(8,128)} fusion(f32[2,3,384,512]{3,2,1,0:T(8,128)} %collective-permute-done.5, f32[2,3,384,512]{3,2,1,0:T(8,128)} %collective-permute-done.4, f32[1,3,3,384,512]{4,3,2,1,0:T(8,128)S(1)} %bitcast.85, f32[1,3,3,384,512]{4,3,2,1,0:T(8,128)S(1)} %bitcast.83), kind=kLoop, calls=%fused_computation.44 | loop fusion | flops 3538944 | bytes 28311552 | tf_op jit(solution)/shard_map/add | solution.py:108
  503.8 4.1 slice_bitcast_fusion.1
  516.2 4.8 all-to-all-start.3
  528.6 4.5 all-to-all-done.3
  533.2 3.5 all-to-all-start.5
  536.7 2.8 fusion.25
  540.3 9.2 %all-to-all-done.5 = bf16[6,8,8,512]{3,2,0,1:T(8,128)(2,1)S(1)} async-done(((bf16[6,8,8,512]{3,2,0,1:T(8,128)(2,1)}), bf16[6,8,8,512]{3,2,0,1:T(8,128)(2,1)S(1)}, u32[]{:S(2)}, u32[]{:S(2)}) %all-to-all-start.5) | async-done | bytes 393248 | tf_op jit(solution)/shard_map/all_to_all | solution.py:116
  549.6 3.5 all-to-all-start.6
  553.8 11.3 %all-to-all-done.6 = bf16[6,8,8,512]{3,2,0,1:T(8,128)(2,1)S(1)} async-done(((bf16[6,8,8,512]{3,2,0,1:T(8,128)(2,1)}), bf16[6,8,8,512]{3,2,0,1:T(8,128)(2,1)S(1)}, u32[]{:S(2)}, u32[]{:S(2)}) %all-to-all-start.6) | async-done | bytes 393248 | tf_op jit(solution)/shard_map/all_to_all | solution.py:117
  565.1 3.5 all-to-all-start.7
  572.4 7.3 %all-to-all-done.7 = bf16[6,8,8,512]{3,2,0,1:T(8,128)(2,1)S(1)} async-done(((bf16[6,8,8,512]{3,2,0,1:T(8,128)(2,1)}), bf16[6,8,8,512]{3,2,0,1:T(8,128)(2,1)S(1)}, u32[]{:S(2)}, u32[]{:S(2)}) %all-to-all-start.7) | async-done | bytes 393248 | tf_op jit(solution)/shard_map/all_to_all | solution.py:118
  (112 shorter events, 56.7 us)
Async XLA Ops:
  9.9 15.9 %copy-start.10 = (bf16[6,2,8,2048]{3,2,1,0:T(8,128)(2,1)S(1)}, bf16[6,2,8,2048]{3,2,1,0:T(8,128)(2,1)}, u32[]{:S(2)}) copy-start(bf16[6,2,8,2048]{3,2,1,0:T(8,128)(2,1)} %param.6) | copy-start | bytes 1179652
  19.5 24.3 %all-to-all-start = ((bf16[4,2,24576]{2,1,0:T(2,128)(2,1)}), bf16[4,2,24576]{2,1,0:T(2,128)(2,1)S(1)}, u32[]{:S(2)}, u32[]{:S(2)}) async-start(bf16[4,2,24576]{2,1,0:T(2,128)(2,1)} %reshape.103), calls=%async_computation | async-start | bytes 786432 | tf_op jit(solution)/shard_map/all_to_all | solution.py:34
  43.8 22.7 %all-to-all-start.1 = ((bf16[4,2,24576]{2,1,0:T(2,128)(2,1)}), bf16[4,2,24576]{2,1,0:T(2,128)(2,1)S(1)}, u32[]{:S(2)}, u32[]{:S(2)}) async-start(bf16[4,2,24576]{2,1,0:T(2,128)(2,1)} %reshape.101), calls=%async_computation.1 | async-start | bytes 786432 | tf_op jit(solution)/shard_map/all_to_all | solution.py:35
  84.2 22.4 %collective-permute-start.1 = (bf16[2,1,1,384,512]{4,3,2,1,0:T(8,128)(2,1)S(1)}, bf16[2,1,1,384,512]{4,3,2,1,0:T(8,128)(2,1)S(1)}, u32[]{:S(2)}, u32[]{:S(2)}) collective-permute-start(bf16[2,1,1,384,512]{4,3,2,1,0:T(8,128)(2,1)S(1)} %pad_maximum_fusion.5), channel_id=1, source_target_pairs={{8,0},{16,8},{24,16},{9,1},{17,9},{25,17},{10,2},{18,10},{26,18},{... | collective-permute-start | bytes 2359304 | tf_op jit(solution)/shard_map/ppermute | solution.py:19
  85.5 21.1 %collective-permute-start = (bf16[2,1,1,384,512]{4,3,2,1,0:T(8,128)(2,1)S(1)}, bf16[2,1,1,384,512]{4,3,2,1,0:T(8,128)(2,1)S(1)}, u32[]{:S(2)}, u32[]{:S(2)}) collective-permute-start(bf16[2,1,1,384,512]{4,3,2,1,0:T(8,128)(2,1)S(1)} %pad_maximum_fusion.5), channel_id=1, source_target_pairs={{0,8},{8,16},{16,24},{1,9},{9,17},{17,25},{2,10},{10,18},{18,26},{... | collective-permute-start | bytes 2359304 | tf_op jit(solution)/shard_map/ppermute | solution.py:18
  108.3 94.2 %collective-permute-start.3 = (bf16[2,3,1,384,512]{4,3,2,1,0:T(8,128)(2,1)}, bf16[2,3,1,384,512]{4,3,2,1,0:T(8,128)(2,1)}, u32[]{:S(2)}, u32[]{:S(2)}) collective-permute-start(bf16[2,3,1,384,512]{4,3,2,1,0:T(8,128)(2,1)} %pad_maximum_fusion.4), channel_id=1, source_target_pairs={{4,0},{5,1},{6,2},{7,3},{12,8},{13,9},{14,10},{15,11},{20,16},{21,... | collective-permute-start | bytes 7077896 | tf_op jit(solution)/shard_map/ppermute | solution.py:19
  109.6 92.9 %collective-permute-start.2 = (bf16[2,3,1,384,512]{4,3,2,1,0:T(8,128)(2,1)}, bf16[2,3,1,384,512]{4,3,2,1,0:T(8,128)(2,1)}, u32[]{:S(2)}, u32[]{:S(2)}) collective-permute-start(bf16[2,3,1,384,512]{4,3,2,1,0:T(8,128)(2,1)} %pad_maximum_fusion.4), channel_id=1, source_target_pairs={{0,4},{1,5},{2,6},{3,7},{8,12},{9,13},{10,14},{11,15},{16,20},{17,... | collective-permute-start | bytes 7077896 | tf_op jit(solution)/shard_map/ppermute | solution.py:18
  125.2 14.7 %copy-start.11 = (bf16[6,2,8,2048]{3,2,1,0:T(8,128)(2,1)S(1)}, bf16[6,2,8,2048]{3,2,1,0:T(8,128)(2,1)}, u32[]{:S(2)}) copy-start(bf16[6,2,8,2048]{3,2,1,0:T(8,128)(2,1)} %param.7) | copy-start | bytes 1179652
  134.8 23.1 %all-to-all-start.2 = ((bf16[4,2,24576]{2,1,0:T(2,128)(2,1)}), bf16[4,2,24576]{2,1,0:T(2,128)(2,1)S(1)}, u32[]{:S(2)}, u32[]{:S(2)}) async-start(bf16[4,2,24576]{2,1,0:T(2,128)(2,1)} %reshape.105), calls=%async_computation.2 | async-start | bytes 786432 | tf_op jit(solution)/shard_map/all_to_all | solution.py:33
  158.0 23.0 %all-to-all-start.4 = ((bf16[4,2,24576]{2,1,0:T(2,128)(2,1)}), bf16[4,2,24576]{2,1,0:T(2,128)(2,1)}, u32[]{:S(2)}, u32[]{:S(2)}) async-start(bf16[4,2,24576]{2,1,0:T(2,128)(2,1)} %reshape.107), calls=%async_computation.4 | async-start | bytes 786432 | tf_op jit(solution)/shard_map/all_to_all | solution.py:36
  180.9 48.7 %copy-start.4 = (bf16[6,4,2,8,512]{4,3,2,1,0:T(8,128)(2,1)}, bf16[6,4,2,8,512]{4,3,2,1,0:T(8,128)(2,1)S(1)}, u32[]{:S(2)}) copy-start(bf16[6,4,2,8,512]{4,3,2,1,0:T(8,128)(2,1)S(1)} %copy.91) | copy-start | bytes 1179652
  201.3 29.3 %copy-start.3 = (bf16[6,4,2,8,512]{4,3,2,1,0:T(8,128)(2,1)}, bf16[6,4,2,8,512]{4,3,2,1,0:T(8,128)(2,1)S(1)}, u32[]{:S(2)}) copy-start(bf16[6,4,2,8,512]{4,3,2,1,0:T(8,128)(2,1)S(1)} %copy.97) | copy-start | bytes 1179652
  206.7 3.4 copy-start.1
  215.8 1.1 copy-start.16
  229.6 3.7 copy-start.5
  233.3 6.5 %copy-start.6 = (bf16[3456,384]{1,0:T(8,128)(2,1)}, bf16[3456,384]{1,0:T(8,128)(2,1)S(1)}, u32[]{:S(2)}) copy-start(bf16[3456,384]{1,0:T(8,128)(2,1)S(1)} %fusion.10) | copy-start | bytes 7962628
  255.8 2.9 copy-start.8
  263.8 232.3 %slice-start = ((s8[7077888]{0:T(1024)(128)(4,1)}), s8[2883584]{0:T(1024)(128)(4,1)S(1)}, s32[]{:S(2)}) async-start(s8[7077888]{0:T(1024)(128)(4,1)} %bitcast.81), calls=%async_computation.8 | async-start | bytes 5767168
  271.9 224.1 %slice-start.1 = ((s8[7077888]{0:T(1024)(128)(4,1)}), s8[4194304]{0:T(1024)(128)(4,1)S(1)}, s32[]{:S(2)}) async-start(s8[7077888]{0:T(1024)(128)(4,1)} %bitcast.81), calls=%async_computation.9 | async-start | bytes 8388608
  271.9 224.2 %copy-start = (f32[3456,512]{1,0:T(8,128)S(1)}, f32[3456,512]{1,0:T(8,128)}, u32[]{:S(2)}) copy-start(f32[3456,512]{1,0:T(8,128)} %copy.105) | copy-start | bytes 21233668
  276.4 114.6 %collective-permute-start.4 = (f32[2,3,384,512]{3,2,1,0:T(8,128)S(1)}, f32[2,3,384,512]{3,2,1,0:T(8,128)}, u32[]{:S(2)}, u32[]{:S(2)}) collective-permute-start(f32[2,3,384,512]{3,2,1,0:T(8,128)S(1)} %get-tuple-element.4), channel_id=1, source_target_pairs={{0,8},{8,16},{16,24},{1,9},{9,17},{17,25},{2,10},{10,18},{18,26},{... | collective-permute-start | bytes 14155784 | tf_op jit(solution)/shard_map/ppermute | solution.py:27
  294.8 201.2 %collective-permute-start.5 = (f32[2,3,384,512]{3,2,1,0:T(8,128)S(1)}, f32[2,3,384,512]{3,2,1,0:T(8,128)}, u32[]{:S(2)}, u32[]{:S(2)}) collective-permute-start(f32[2,3,384,512]{3,2,1,0:T(8,128)S(1)} %get-tuple-element.5), channel_id=1, source_target_pairs={{8,0},{16,8},{24,16},{9,1},{17,9},{25,17},{10,2},{18,10},{26,18},{... | collective-permute-start | bytes 14155784 | tf_op jit(solution)/shard_map/ppermute | solution.py:27
  503.8 7.9 %copy-start.12 = (bf16[384,128]{0,1:T(8,128)(2,1)S(1)}, bf16[384,128]{0,1:T(8,128)(2,1)}, u32[]{:S(2)}) copy-start(bf16[384,128]{0,1:T(8,128)(2,1)} %get-tuple-element.31) | copy-start | bytes 294916
  503.8 7.9 %copy-start.13 = (bf16[384,128]{0,1:T(8,128)(2,1)S(1)}, bf16[384,128]{0,1:T(8,128)(2,1)}, u32[]{:S(2)}) copy-start(bf16[384,128]{0,1:T(8,128)(2,1)} %get-tuple-element.27) | copy-start | bytes 294916
  503.8 7.9 %copy-start.14 = (bf16[384,128]{0,1:T(8,128)(2,1)S(1)}, bf16[384,128]{0,1:T(8,128)(2,1)}, u32[]{:S(2)}) copy-start(bf16[384,128]{0,1:T(8,128)(2,1)} %get-tuple-element.29) | copy-start | bytes 294916
  503.8 7.9 %copy-start.15 = (bf16[384,128]{0,1:T(8,128)(2,1)S(1)}, bf16[384,128]{0,1:T(8,128)(2,1)}, u32[]{:S(2)}) copy-start(bf16[384,128]{0,1:T(8,128)(2,1)} %get-tuple-element.25) | copy-start | bytes 294916
  503.8 17.2 %copy-start.2 = (bf16[1,3,3,384,512]{4,3,2,1,0:T(8,128)(2,1)S(1)}, bf16[1,3,3,384,512]{4,3,2,1,0:T(8,128)(2,1)}, u32[]{:S(2)}) copy-start(bf16[1,3,3,384,512]{4,3,2,1,0:T(8,128)(2,1)} %copy-done.1) | copy-start | bytes 10616836
  507.9 28.7 %collective-permute-start.6 = (f32[2,384,512]{2,1,0:T(8,128)}, f32[2,384,512]{2,1,0:T(8,128)}, u32[]{:S(2)}, u32[]{:S(2)}) collective-permute-start(f32[2,384,512]{2,1,0:T(8,128)} %get-tuple-element.8), channel_id=1, source_target_pairs={{0,4},{1,5},{2,6},{3,7},{8,12},{9,13},{10,14},{11,15},{16,20},{17,... | collective-permute-start | bytes 4718600 | tf_op jit(solution)/shard_map/ppermute | solution.py:27
  510.3 26.3 %collective-permute-start.7 = (f32[2,384,512]{2,1,0:T(8,128)}, f32[2,384,512]{2,1,0:T(8,128)}, u32[]{:S(2)}, u32[]{:S(2)}) collective-permute-start(f32[2,384,512]{2,1,0:T(8,128)} %get-tuple-element.9), channel_id=1, source_target_pairs={{4,0},{5,1},{6,2},{7,3},{12,8},{13,9},{14,10},{15,11},{20,16},{21,... | collective-permute-start | bytes 4718600 | tf_op jit(solution)/shard_map/ppermute | solution.py:27
  516.2 17.0 %all-to-all-start.3 = ((bf16[6,8,8,512]{3,2,0,1:T(8,128)(2,1)}), bf16[6,8,8,512]{3,2,0,1:T(8,128)(2,1)}, u32[]{:S(2)}, u32[]{:S(2)}) async-start(bf16[6,8,8,512]{3,2,0,1:T(8,128)(2,1)} %copy.93), calls=%async_computation.3 | async-start | bytes 786432 | tf_op jit(solution)/shard_map/all_to_all | solution.py:115
  521.0 5.2 copy-start.9
  523.6 3.3 copy-start.7
  533.2 16.4 %all-to-all-start.5 = ((bf16[6,8,8,512]{3,2,0,1:T(8,128)(2,1)}), bf16[6,8,8,512]{3,2,0,1:T(8,128)(2,1)S(1)}, u32[]{:S(2)}, u32[]{:S(2)}) async-start(bf16[6,8,8,512]{3,2,0,1:T(8,128)(2,1)} %copy.103), calls=%async_computation.5 | async-start | bytes 786432 | tf_op jit(solution)/shard_map/all_to_all | solution.py:116
  549.6 15.5 %all-to-all-start.6 = ((bf16[6,8,8,512]{3,2,0,1:T(8,128)(2,1)}), bf16[6,8,8,512]{3,2,0,1:T(8,128)(2,1)S(1)}, u32[]{:S(2)}, u32[]{:S(2)}) async-start(bf16[6,8,8,512]{3,2,0,1:T(8,128)(2,1)} %copy.111), calls=%async_computation.6 | async-start | bytes 786432 | tf_op jit(solution)/shard_map/all_to_all | solution.py:117
  565.1 14.7 %all-to-all-start.7 = ((bf16[6,8,8,512]{3,2,0,1:T(8,128)(2,1)}), bf16[6,8,8,512]{3,2,0,1:T(8,128)(2,1)S(1)}, u32[]{:S(2)}, u32[]{:S(2)}) async-start(bf16[6,8,8,512]{3,2,0,1:T(8,128)(2,1)} %copy.114), calls=%async_computation.7 | async-start | bytes 786432 | tf_op jit(solution)/shard_map/all_to_all | solution.py:118
where the time goes:
time: 591 us; the launch traced here: 582 us
  waiting for transfers between devices  249 us (42%)
  local copies, waits for them, and re-layouts  181 us (31%)
  starting transfers between devices  73.8 us (12%)
  matrix products  45.3 us (8%)
  other arithmetic  31.1 us (5%)
    ppermute x4, waiting for transfers between devices, shifted(): return lax.ppermute(value, axis, pairs)  200 us
    unnamed x55, local copies, waits for them, and re-layouts  114 us
    ppermute x4, starting transfers between devices, shifted(): return lax.ppermute(value, axis, pairs)  23.4 us
    ppermute x2, waiting for transfers between devices, padded(): after = lax.ppermute(leading, axis, down)  16.5 us
    dot_general x4, matrix products, body(): jnp.einsum('qd,kd->qk', grad_rows, value_rows, preferred_element_type=jnp...  14.4 us
  transfers between devices with their start and end apart: 16, of which 7 were waited for; matrix products, arithmetic and copies ran while one was open for 23% of the time, Pallas kernels for 0%

commit v1 on v0

v1 whole, which is shorter than its diff:
```python
import functools
import math

import jax
import jax.numpy as jnp
from jax import lax
from jax.experimental import pallas as pl
from jax.experimental.pallas import tpu as pltpu
from jax.sharding import PartitionSpec as P

DH = 128
LOW = -1e30


def neighbours(axis, size):
    me = lax.axis_index(axis)
    if size == 1:
        return []
    if size == 2:
        return [(1 - me, None, 1)]
    return [(me - 1, me > 0, 2), (me + 1, me < size - 1, 1)]


def guarded(valid, fn):
    if valid is None:
        fn()
    else:
        pl.when(valid)(fn)


def kernel(
    sizes,
    rows,
    heads,
    q_ref,
    k_ref,
    v_ref,
    g_ref,
    o_ref,
    dq_ref,
    dk_ref,
    dv_ref,
    qg,
    win,
    s_ref,
    outb,
    own,
    r1s,
    r1r,
    r2s,
    r2r,
    in_s,
    in_r,
    ht_s,
    ht_r,
    hh_s,
    hh_r,
    a1_s,
    a1_r,
    a2_s,
    a2_r,
    ou_s,
    ou_r,
):
    size_t, size_h, size_z = sizes
    tokens = rows * size_z
    z = lax.axis_index("head")
    times = neighbours("ta", size_t)
    sides = neighbours("ha", size_h)
    nt, nr = 1 + len(times), 1 + len(sides)
    factor = 1.0 / math.sqrt(DH)
    scale = factor * math.log2(math.e)

    barrier = pltpu.get_barrier_semaphore()
    expected = size_z - 1
    for d in range(1, size_z):
        pl.semaphore_signal(barrier, inc=1, device_id={"head": lax.rem(z + d, size_z)}, device_id_type=pl.DeviceIdType.MESH)
    for axis, near in (("ta", times), ("ha", sides)):
        for peer, valid, _ in near:

            def greet(axis=axis, peer=peer):
                pl.semaphore_signal(barrier, inc=1, device_id={axis: peer}, device_id_type=pl.DeviceIdType.MESH)

            guarded(valid, greet)
            expected = expected + (1 if valid is None else jnp.where(valid, 1, 0))
    pl.semaphore_wait(barrier, expected)

    def columns(group, h):
        return pl.ds(pl.multiple_of((group * heads + h) * DH, DH), DH)

    def part(group):
        return pl.ds(pl.multiple_of(group * rows, rows), rows)

    ins = (k_ref, v_ref, q_ref, g_ref)
    outs = (o_ref, dq_ref, dk_ref, dv_ref)

    def landing(h, a, group):
        if a < 2:
            return win.at[h, 0, 0, a, part(group), :]
        return qg.at[h, a - 2, part(group), :]

    def in_copy(h, a, d):
        peer = lax.rem(z + d, size_z)
        return pltpu.make_async_remote_copy(
            src_ref=ins[a].at[:, columns(peer, h)],
            dst_ref=landing(h, a, z),
            send_sem=in_s.at[h, a, d],
            recv_sem=in_r.at[h, a, d],
            device_id={"head": peer},
            device_id_type=pl.DeviceIdType.MESH,
        )

    def out_copy(h, a, d):
        peer = lax.rem(z + d, size_z)
        return pltpu.make_async_remote_copy(
            src_ref=outb.at[h, a, part(peer), :],
            dst_ref=outs[a].at[:, columns(z, h)],
            send_sem=ou_s.at[h, a, d],
            recv_sem=ou_r.at[h, a, d],
            device_id={"head": peer},
            device_id_type=pl.DeviceIdType.MESH,
        )

    def side_copy(axis, src, dst, send, recv, peer):
        return pltpu.make_async_remote_copy(
            src_ref=src,
            dst_ref=dst,
            send_sem=send,
            recv_sem=recv,
            device_id={axis: peer},
            device_id_type=pl.DeviceIdType.MESH,
        )

    def halo_t(h, i):
        peer, _, there = times[i]
        return side_copy("ta", win.at[h, 0, 0], win.at[h, 0, there], ht_s.at[h, i], ht_r.at[h, there - 1], peer)

    def halo_h(h, i):
        peer, _, there = sides[i]
        return side_copy("ha", win.at[h, 0], win.at[h, there], hh_s.at[h, i], hh_r.at[h, there - 1], peer)

    def back_h(h, i):
        peer, _, there = sides[i]
        return side_copy("ha", r1s.at[h, i], r1r.at[h, there - 1], a1_s.at[h, i], a1_r.at[h, there - 1], peer)

    def back_t(h, i):
        peer, _, there = times[i]
        return side_copy("ta", r2s.at[h, i], r2r.at[h, there - 1], a2_s.at[h, i], a2_r.at[h, there - 1], peer)

    def arrival(axis, dst, recv, peer):
        return side_copy(axis, dst, dst, recv, recv, peer)

    for i, (peer, valid, _) in enumerate(times):
        if valid is not None:

            @pl.when(jnp.logical_not(valid))
            def _(i=i):
                @pl.loop(0, heads)
                def _(h):
                    win[h, 0, i + 1] = jnp.zeros((2, tokens, DH), win.dtype)

    for i, (peer, valid, _) in enumerate(sides):
        if valid is not None:

            @pl.when(jnp.logical_not(valid))
            def _(i=i):
                @pl.loop(0, heads)
                def _(h):
                    win[h, i + 1] = jnp.zeros((nt, 2, tokens, DH), win.dtype)

    @pl.loop(0, heads)
    def _(h):
        for a in range(4):
            for d in range(1, size_z):
                in_copy(h, a, d).start()
        for a in range(4):
            landing(h, a, z)[...] = ins[a][:, columns(z, h)]

    def send_times(h):
        for a in range(2):
            for d in range(1, size_z):
                in_copy(h, a, d).wait_recv()
        for i, (peer, valid, _) in enumerate(times):
            guarded(valid, lambda i=i: halo_t(h, i).start())

    def send_sides(h):
        for i, (peer, valid, _) in enumerate(times):
            guarded(valid, lambda i=i, peer=peer: arrival("ta", win.at[h, 0, i + 1], ht_r.at[h, i], peer).wait_recv())
        for i, (peer, valid, _) in enumerate(sides):
            guarded(valid, lambda i=i: halo_h(h, i).start())

    def attend(h):
        for a in range(2, 4):
            for d in range(1, size_z):
                in_copy(h, a, d).wait_recv()
        queries = qg[h, 0]
        grads = qg[h, 1]
        highest = jnp.full((1, tokens), LOW, jnp.float32)
        for r in range(nr):
            if r > 0:
                peer, valid, _ = sides[r - 1]
                guarded(valid, lambda r=r, peer=peer: arrival("ha", win.at[h, r], hh_r.at[h, r - 1], peer).wait_recv())
            for t in range(nt):
                scores = lax.dot_general(win[h, r, t, 0], queries, (((1,), (1,)), ((), ())), preferred_element_type=jnp.float32) * scale
                for cond in ([times[t - 1][1]] if t > 0 else []) + ([sides[r - 1][1]] if r > 0 else []):
                    if cond is not None:
                        scores = jnp.where(cond, scores, LOW)
                s_ref[r * nt + t] = scores
                highest = jnp.maximum(highest, jnp.max(scores, axis=0, keepdims=True))
        total = jnp.zeros((1, tokens), jnp.float32)
        mixed = jnp.zeros((DH, tokens), jnp.float32)
        for r in range(nr):
            for t in range(nt):
                weights = jnp.exp2(s_ref[r * nt + t] - highest)
                s_ref[r * nt + t] = weights
                total = total + jnp.sum(weights, axis=0, keepdims=True)
                mixed = mixed + lax.dot_general(
                    win[h, r, t, 1], weights.astype(jnp.bfloat16), (((0,), (0,)), ((), ())), preferred_element_type=jnp.float32
                )
        inverse = 1.0 / total
        attended = jnp.transpose(mixed * inverse).astype(jnp.bfloat16)
        outb[h, 0] = attended
        products = grads.astype(jnp.float32) * attended.astype(jnp.float32)
        row_dot = jnp.sum(jnp.transpose(products), axis=0, keepdims=True)
        for d in range(1, size_z):
            out_copy(h, 0, d).start()
        query_grad = jnp.zeros((DH, tokens), jnp.float32)
        for r in reversed(range(nr)):
            for t in range(nt):
                keys, values = win[h, r, t, 0], win[h, r, t, 1]
                probs = s_ref[r * nt + t] * inverse
                value_term = jnp.dot(probs.astype(jnp.bfloat16), grads, preferred_element_type=jnp.float32)
                prob_grad = lax.dot_general(values, grads, (((1,), (1,)), ((), ())), preferred_element_type=jnp.float32)
                score_grad = (probs * (prob_grad - row_dot)).astype(jnp.bfloat16)
                query_grad = query_grad + lax.dot_general(
                    keys, score_grad, (((0,), (0,)), ((), ())), preferred_element_type=jnp.float32
                )
                key_term = jnp.dot(score_grad, queries, preferred_element_type=jnp.float32) * factor
                if r == 0:
                    own[h, t, 0] = key_term
                    own[h, t, 1] = value_term
                else:
                    r1s[h, r - 1, t, 0] = key_term.astype(jnp.bfloat16)
                    r1s[h, r - 1, t, 1] = value_term.astype(jnp.bfloat16)
            if r > 0:
                guarded(sides[r - 1][1], lambda r=r: back_h(h, r - 1).start())
        outb[h, 1] = jnp.transpose(query_grad * factor).astype(jnp.bfloat16)
        for d in range(1, size_z):
            out_copy(h, 1, d).start()

    def return_times(h):
        for i, (peer, valid, _) in enumerate(sides):

            def fold(i=i, peer=peer):
                arrival("ha", r1r.at[h, i], a1_r.at[h, i], peer).wait_recv()
                for t in range(nt):
                    own[h, t] = own[h, t] + r1r[h, i, t].astype(jnp.float32)

            guarded(valid, fold)
        for i, (peer, valid, _) in enumerate(times):

            def send(i=i):
                r2s[h, i] = own[h, i + 1].astype(jnp.bfloat16)
                back_t(h, i).start()

            guarded(valid, send)

    def finish(h):
        for i, (peer, valid, _) in enumerate(times):

            def fold(i=i, peer=peer):
                arrival("ta", r2r.at[h, i], a2_r.at[h, i], peer).wait_recv()
                own[h, 0] = own[h, 0] + r2r[h, i].astype(jnp.float32)

            guarded(valid, fold)
        outb[h, 2] = own[h, 0, 0].astype(jnp.bfloat16)
        outb[h, 3] = own[h, 0, 1].astype(jnp.bfloat16)
        for a in range(2, 4):
            for d in range(1, size_z):
                out_copy(h, a, d).start()
        for a in range(4):
            outs[a][:, columns(z, h)] = outb[h, a, part(z), :]

    send_times(0)

    @pl.loop(0, heads)
    def _(h):
        pl.when(h + 1 < heads)(lambda: send_times(h + 1))
        send_sides(h)
        attend(h)
        return_times(h)
        pl.when(h > 0)(lambda: finish(h - 1))

    finish(heads - 1)

    @pl.loop(0, heads)
    def _(h):
        for a in range(4):
            for d in range(1, size_z):
                in_copy(h, a, d).wait_send()
                out_copy(h, a, d).wait_recv()
                out_copy(h, a, d).wait_send()
        for i, (peer, valid, _) in enumerate(times):
            guarded(valid, lambda i=i: halo_t(h, i).wait_send())
            guarded(valid, lambda i=i: back_t(h, i).wait_send())
        for i, (peer, valid, _) in enumerate(sides):
            guarded(valid, lambda i=i: halo_h(h, i).wait_send())
            guarded(valid, lambda i=i: back_h(h, i).wait_send())


def body(queries, keys, values, out_grad):
    sizes = tuple(lax.axis_size(axis) for axis in ("ta", "ha", "head"))
    size_t, size_h, size_z = sizes
    shape = queries.shape
    rows = shape[0] * shape[1] * shape[2]
    width = shape[3]
    heads = width // DH // size_z
    tokens = rows * size_z
    nt, nr = min(3, size_t), min(3, size_h)
    bf16 = jnp.bfloat16
    dma = pltpu.SemaphoreType.DMA
    mt, mr = max(1, nt - 1), max(1, nr - 1)
    flat = [x.reshape(rows, width) for x in (queries, keys, values, out_grad)]
    outs = pl.pallas_call(
        functools.partial(kernel, sizes, rows, heads),
        out_shape=[jax.ShapeDtypeStruct((rows, width), bf16)] * 4,
        in_specs=[pl.BlockSpec(memory_space=pltpu.VMEM)] * 4,
        out_specs=[pl.BlockSpec(memory_space=pltpu.VMEM)] * 4,
        scratch_shapes=[
            pltpu.VMEM((heads, 2, tokens, DH), bf16),
            pltpu.VMEM((heads, nr, nt, 2, tokens, DH), bf16),
            pltpu.VMEM((nr * nt, tokens, tokens), jnp.float32),
            pltpu.VMEM((heads, 4, tokens, DH), bf16),
            pltpu.VMEM((heads, nt, 2, tokens, DH), jnp.float32),
            pltpu.VMEM((heads, mr, nt, 2, tokens, DH), bf16),
            pltpu.VMEM((heads, mr, nt, 2, tokens, DH), bf16),
            pltpu.VMEM((heads, mt, 2, tokens, DH), bf16),
            pltpu.VMEM((heads, mt, 2, tokens, DH), bf16),
            dma((heads, 4, size_z)),
            dma((heads, 4, size_z)),
            dma((heads, mt)),
            dma((heads, mt)),
            dma((heads, mr)),
            dma((heads, mr)),
            dma((heads, mr)),
            dma((heads, mr)),
            dma((heads, mt)),
            dma((heads, mt)),
            dma((heads, 4, size_z)),
            dma((heads, 4, size_z)),
        ],
        compiler_params=pltpu.CompilerParams(collective_id=0, has_side_effects=True, vmem_limit_bytes=56 * 1024 * 1024),
        name="tile_attention",
    )(*flat)
    return tuple(x.reshape(shape) for x in outs)


def solution(mesh):
    spec = P("ta", ("ha", "head"), None, None)
    return jax.shard_map(body, mesh=mesh, in_specs=(spec,) * 4, out_specs=(spec,) * 4, check_vma=False)
```

time: 591 us -> 99.6 us (0.17)
  the two profiles are of different devices: /device:TPU:0 before, /device:TPU:4 now
where the time goes in v1:
time: 99.6 us; the launch traced here: 99.3 us
  Pallas kernels  93.8 us (94%)
  local copies, waits for them, and re-layouts  4.84 us (5%)
    pallas_call x1, Pallas kernels, body(): pl.pallas_call(functools.partial(kernel, sizes, rows, heads), out_shape=[...  93.8 us
    unnamed x10, local copies, waits for them, and re-layouts  4.84 us

profile of v1, /device:TPU:4, one launch (start us, length us, event | category | flops | bytes accessed | tf_op | source)
XLA Modules:
  0.0 99.3 jit_solution(12330290588445313057)
XLA Ops:
  0.6 93.8 %tile_attention.1 = (bf16[96,2048]{1,0:T(8,128)(2,1)}, bf16[96,2048]{1,0:T(8,128)(2,1)}, bf16[96,2048]{1,0:T(8,128)(2,1)}, bf16[96,2048]{1,0:T(8,128)(2,1)}) custom-call(bf16[96,2048]{1,0:T(8,128)(2,1)} %bitcast.12, bf16[96,2048]{1,0:T(8,128)(2,1)} %bitcast.13, bf16[96,2048]{1,0:T(8,128)(2,1)} %bitcast.14, bf16[96,2048]{1,0:T(8,128)(2,1)} %bitcast.15), custom_call_target="tpu_custom_call" | custom-call | tf_op jit(solution)/shard_map/tile_attention/pallas_call | solution.py:324
  94.4 0.0 copy-start.2
  94.5 1.8 %copy.12 = bf16[6,2,8,2048]{3,2,1,0:T(8,128)(2,1)} copy(bf16[6,2,8,2048]{3,2,1,0:T(8,128)(2,1)} %bitcast.11) | data formatting | bytes 786432
  96.3 0.0 copy-done.2
  96.3 0.0 copy-start.1
  96.3 0.7 copy.13
  97.0 0.4 copy-done.1
  97.4 0.0 copy-start
  97.4 0.7 copy.14
  98.2 0.4 copy-done
  98.6 0.7 copy.15
Async XLA Ops:
  94.4 1.8 %copy-start.2 = (bf16[96,2048]{1,0:T(8,128)(2,1)S(1)}, bf16[96,2048]{1,0:T(8,128)(2,1)}, u32[]{:S(2)}) copy-start(bf16[96,2048]{1,0:T(8,128)(2,1)} %get-tuple-element.9) | copy-start | bytes 1179652
  96.3 1.1 %copy-start.1 = (bf16[96,2048]{1,0:T(8,128)(2,1)S(1)}, bf16[96,2048]{1,0:T(8,128)(2,1)}, u32[]{:S(2)}) copy-start(bf16[96,2048]{1,0:T(8,128)(2,1)} %get-tuple-element.10) | copy-start | bytes 1179652
  97.4 1.1 %copy-start = (bf16[96,2048]{1,0:T(8,128)(2,1)S(1)}, bf16[96,2048]{1,0:T(8,128)(2,1)}, u32[]{:S(2)}) copy-start(bf16[96,2048]{1,0:T(8,128)(2,1)} %get-tuple-element.11) | copy-start | bytes 1179652

commit v2 on v1

--- a/solution.py
+++ b/solution.py
@@ -68,6 +68,13 @@
     times = neighbours("ta", size_t)
     sides = neighbours("ha", size_h)
     nt, nr = 1 + len(times), 1 + len(sides)
+    relay = size_t == 4
+    step = lax.axis_index("ta")
+    across, along = step + 1 - 2 * lax.rem(step, 2), lax.rem(step + 2, 4)
+    near, far = 2 - lax.rem(step, 2), 1 + lax.rem(step, 2)
+    inner = (step == 1) | (step == 2)
+    outer = jnp.logical_not(inner)
+    greeted = [(across, None, None), (along, None, None)] if relay else times
     factor = 1.0 / math.sqrt(DH)
     scale = factor * math.log2(math.e)
 
@@ -75,8 +82,8 @@
     expected = size_z - 1
     for d in range(1, size_z):
         pl.semaphore_signal(barrier, inc=1, device_id={"head": lax.rem(z + d, size_z)}, device_id_type=pl.DeviceIdType.MESH)
-    for axis, near in (("ta", times), ("ha", sides)):
-        for peer, valid, _ in near:
+    for axis, group in (("ta", greeted), ("ha", sides)):
+        for peer, valid, _ in group:
 
             def greet(axis=axis, peer=peer):
                 pl.semaphore_signal(barrier, inc=1, device_id={axis: peer}, device_id_type=pl.DeviceIdType.MESH)
@@ -135,6 +142,18 @@
         peer, _, there = times[i]
         return side_copy("ta", win.at[h, 0, 0], win.at[h, 0, there], ht_s.at[h, i], ht_r.at[h, there - 1], peer)
 
+    def halo_across(h):
+        return side_copy("ta", win.at[h, 0, 0], win.at[h, 0, far], ht_s.at[h, 0], ht_r.at[h, far - 1], across)
+
+    def halo_along(h):
+        return side_copy("ta", win.at[h, 0, near], win.at[h, 0, far], ht_s.at[h, 1], ht_r.at[h, far - 1], along)
+
+    def back_across(h):
+        return side_copy("ta", r2s.at[h, 0], r2r.at[h, 0], a2_s.at[h, 0], a2_r.at[h, 0], across)
+
+    def back_along(h):
+        return side_copy("ta", r2s.at[h, 1], r2r.at[h, 1], a2_s.at[h, 1], a2_r.at[h, 1], along)
+
     def halo_h(h, i):
         peer, _, there = sides[i]
         return side_copy("ha", win.at[h, 0], win.at[h, there], hh_s.at[h, i], hh_r.at[h, there - 1], peer)
@@ -168,11 +187,20 @@
                 def _(h):
                     win[h, i + 1] = jnp.zeros((nt, 2, tokens, DH), win.dtype)
 
+    def send_in(h, first):
+        for a in (first, first + 1):
+            for d in range(1, size_z):
+                in_copy(h, a, d).start()
+
+    send_in(0, 0)
+
     @pl.loop(0, heads)
     def _(h):
-        for a in range(4):
-            for d in range(1, size_z):
-                in_copy(h, a, d).start()
+        pl.when(h + 1 < heads)(lambda: send_in(h + 1, 0))
+        send_in(h, 2)
+
+    @pl.loop(0, heads)
+    def _(h):
         for a in range(4):
             landing(h, a, z)[...] = ins[a][:, columns(z, h)]
 
@@ -180,16 +208,27 @@
         for a in range(2):
             for d in range(1, size_z):
                 in_copy(h, a, d).wait_recv()
+        if relay:
+            halo_across(h).start()
+            return
         for i, (peer, valid, _) in enumerate(times):
             guarded(valid, lambda i=i: halo_t(h, i).start())
 
+    def pass_on(h):
+        if relay:
+            arrival("ta", win.at[h, 0, near], ht_r.at[h, near - 1], across).wait_recv()
+            pl.when(outer)(lambda: halo_along(h).start())
+
     def send_sides(h):
-        for i, (peer, valid, _) in enumerate(times):
-            guarded(valid, lambda i=i, peer=peer: arrival("ta", win.at[h, 0, i + 1], ht_r.at[h, i], peer).wait_recv())
+        if relay:
+            pl.when(inner)(lambda: arrival("ta", win.at[h, 0, far], ht_r.at[h, far - 1], along).wait_recv())
+        else:
+            for i, (peer, valid, _) in enumerate(times):
+                guarded(valid, lambda i=i, peer=peer: arrival("ta", win.at[h, 0, i + 1], ht_r.at[h, i], peer).wait_recv())
         for i, (peer, valid, _) in enumerate(sides):
             guarded(valid, lambda i=i: halo_h(h, i).start())
 
-    def attend(h):
+    def attend(h, between):
         for a in range(2, 4):
             for d in range(1, size_z):
                 in_copy(h, a, d).wait_recv()
@@ -224,6 +263,7 @@
         row_dot = jnp.sum(jnp.transpose(products), axis=0, keepdims=True)
         for d in range(1, size_z):
             out_copy(h, 0, d).start()
+        between()
         query_grad = jnp.zeros((DH, tokens), jnp.float32)
         for r in reversed(range(nr)):
             for t in range(nt):
@@ -257,6 +297,16 @@
                     own[h, t] = own[h, t] + r1r[h, i, t].astype(jnp.float32)
 
             guarded(valid, fold)
+        if relay:
+
+            @pl.when(inner)
+            def _():
+                r2s[h, 1] = own[h, far].astype(jnp.bfloat16)
+                back_along(h).start()
+                r2s[h, 0] = own[h, near].astype(jnp.bfloat16)
+                back_across(h).start()
+
+            return
         for i, (peer, valid, _) in enumerate(times):
 
             def send(i=i):
@@ -265,14 +315,27 @@
 
             guarded(valid, send)
 
+    def pass_back(h):
+        if relay:
+
+            @pl.when(outer)
+            def _():
+                arrival("ta", r2r.at[h, 1], a2_r.at[h, 1], along).wait_recv()
+                r2s[h, 0] = (own[h, near] + r2r[h, 1].astype(jnp.float32)).astype(jnp.bfloat16)
+                back_across(h).start()
+
     def finish(h):
-        for i, (peer, valid, _) in enumerate(times):
-
-            def fold(i=i, peer=peer):
-                arrival("ta", r2r.at[h, i], a2_r.at[h, i], peer).wait_recv()
-                own[h, 0] = own[h, 0] + r2r[h, i].astype(jnp.float32)
-
-            guarded(valid, fold)
+        if relay:
+            arrival("ta", r2r.at[h, 0], a2_r.at[h, 0], across).wait_recv()
+            own[h, 0] = own[h, 0] + r2r[h, 0].astype(jnp.float32)
+        else:
+            for i, (peer, valid, _) in enumerate(times):
+
+                def fold(i=i, peer=peer):
+                    arrival("ta", r2r.at[h, i], a2_r.at[h, i], peer).wait_recv()
+                    own[h, 0] = own[h, 0] + r2r[h, i].astype(jnp.float32)
+
+                guarded(valid, fold)
         outb[h, 2] = own[h, 0, 0].astype(jnp.bfloat16)
         outb[h, 3] = own[h, 0, 1].astype(jnp.bfloat16)
         for a in range(2, 4):
@@ -282,15 +345,18 @@
             outs[a][:, columns(z, h)] = outb[h, a, part(z), :]
 
     send_times(0)
+    pass_on(0)
 
     @pl.loop(0, heads)
     def _(h):
         pl.when(h + 1 < heads)(lambda: send_times(h + 1))
         send_sides(h)
-        attend(h)
+        pl.when(h + 1 < heads)(lambda: pass_on(h + 1))
+        pl.when(h > 0)(lambda: pass_back(h - 1))
+        attend(h, lambda: pl.when(h > 0)(lambda: finish(h - 1)))
         return_times(h)
-        pl.when(h > 0)(lambda: finish(h - 1))
-
+
+    pass_back(heads - 1)
     finish(heads - 1)
 
     @pl.loop(0, heads)
@@ -300,9 +366,15 @@
                 in_copy(h, a, d).wait_send()
                 out_copy(h, a, d).wait_recv()
                 out_copy(h, a, d).wait_send()
-        for i, (peer, valid, _) in enumerate(times):
-            guarded(valid, lambda i=i: halo_t(h, i).wait_send())
-            guarded(valid, lambda i=i: back_t(h, i).wait_send())
+        if relay:
+            halo_across(h).wait_send()
+            back_across(h).wait_send()
+            pl.when(outer)(lambda: halo_along(h).wait_send())
+            pl.when(inner)(lambda: back_along(h).wait_send())
+        else:
+            for i, (peer, valid, _) in enumerate(times):
+                guarded(valid, lambda i=i: halo_t(h, i).wait_send())
+                guarded(valid, lambda i=i: back_t(h, i).wait_send())
         for i, (peer, valid, _) in enumerate(sides):
             guarded(valid, lambda i=i: halo_h(h, i).wait_send())
             guarded(valid, lambda i=i: back_h(h, i).wait_send())

time: 99.6 us -> 114 us (1.14)
  Pallas kernels: 93.8 us -> 108 us
    pallas_call x1, Pallas kernels: 93.8 us -> 108 us  [body(): pl.pallas_call(functools.partial(kernel, sizes, rows, heads), out_shape=[...]
where the time goes in v2:
time: 114 us
  Pallas kernels  108 us (95%)
  local copies, waits for them, and re-layouts  4.84 us (4%)
    pallas_call x1, Pallas kernels, body(): pl.pallas_call(functools.partial(kernel, sizes, rows, heads), out_shape=[...  108 us
    unnamed x10, local copies, waits for them, and re-layouts  4.84 us

profile of v2, /device:TPU:4, one launch (start us, length us, event | category | flops | bytes accessed | tf_op | source)
XLA Modules:
  0.0 114.0 jit_solution(3073154327787206329)
XLA Ops:
  0.6 108.5 %tile_attention.1 = (bf16[96,2048]{1,0:T(8,128)(2,1)}, bf16[96,2048]{1,0:T(8,128)(2,1)}, bf16[96,2048]{1,0:T(8,128)(2,1)}, bf16[96,2048]{1,0:T(8,128)(2,1)}) custom-call(bf16[96,2048]{1,0:T(8,128)(2,1)} %bitcast.12, bf16[96,2048]{1,0:T(8,128)(2,1)} %bitcast.13, bf16[96,2048]{1,0:T(8,128)(2,1)} %bitcast.14, bf16[96,2048]{1,0:T(8,128)(2,1)} %bitcast.15), custom_call_target="tpu_custom_call" | custom-call | tf_op jit(solution)/shard_map/tile_attention/pallas_call | solution.py:396
  109.1 0.0 copy-start.2
  109.1 1.8 %copy.12 = bf16[6,2,8,2048]{3,2,1,0:T(8,128)(2,1)} copy(bf16[6,2,8,2048]{3,2,1,0:T(8,128)(2,1)} %bitcast.11) | data formatting | bytes 786432
  110.9 0.0 copy-done.2
  111.0 0.0 copy-start.1
  111.0 0.7 copy.13
  111.7 0.4 copy-done.1
  112.1 0.0 copy-start
  112.1 0.7 copy.14
  112.8 0.4 copy-done
  113.2 0.7 copy.15
Async XLA Ops:
  109.1 1.8 %copy-start.2 = (bf16[96,2048]{1,0:T(8,128)(2,1)S(1)}, bf16[96,2048]{1,0:T(8,128)(2,1)}, u32[]{:S(2)}) copy-start(bf16[96,2048]{1,0:T(8,128)(2,1)} %get-tuple-element.9) | copy-start | bytes 1179652
  111.0 1.1 copy-start.1
  112.1 1.1 copy-start
